TPU v7x, 128 devices: a whole 4x4x4 slice. The times are simulated.
128 devices in a mesh: seq: 32 (over x, y, core), tp: 4 (over z).
Axes of the slice: x: 4, y: 4, z: 4, core: 2. Of those that a mesh axis runs over, the one named last changes fastest.
Arguments:
- inputs: float32 [8192, 1024], P('seq', 'tp'), may hold values from -6 to 6
- cotangent: float32 [8192, 1024], P('seq', 'tp'), may hold values from -6 to 6
- entry_weight: float32 [2, 3, 1024, 1024], P(None, None, 'seq', 'tp'), may hold values from -0.1875 to 0.1875
- exit_weight: float32 [2, 1024, 1024], P(None, 'tp', 'seq'), may hold values from -0.1875 to 0.1875
- gate_up: float32 [2, 2, 1024, 4608], P(None, None, 'seq', 'tp'), may hold values from -0.1875 to 0.1875
- down_weight: float32 [2, 4608, 1024], P(None, 'tp', 'seq'), may hold values from -0.1875 to 0.1875
- conv_kernel: float32 [2, 3, 1024], P(None, None, 'tp'), may hold values from -3 to 3
- norm_gain: float32 [2, 2, 1024], P(None, None, 'tp'), may hold values from 0.5 to 1.5
- entry_first: float32 [2, 3, 1024, 1024], P(None, None, 'seq', 'tp'), may hold values from -27.1529 to 27.1529
- entry_second: float32 [2, 3, 1024, 1024], P(None, None, 'seq', 'tp'), may hold values from 0.8192 to 16.384
- exit_first: float32 [2, 1024, 1024], P(None, 'tp', 'seq'), may hold values from -27.1529 to 27.1529
- exit_second: float32 [2, 1024, 1024], P(None, 'tp', 'seq'), may hold values from 0.8192 to 16.384
- gate_first: float32 [2, 2, 1024, 4608], P(None, None, 'seq', 'tp'), may hold values from -27.1529 to 27.1529
- gate_second: float32 [2, 2, 1024, 4608], P(None, None, 'seq', 'tp'), may hold values from 0.8192 to 16.384
- down_first: float32 [2, 4608, 1024], P(None, 'tp', 'seq'), may hold values from -27.1529 to 27.1529
- down_second: float32 [2, 4608, 1024], P(None, 'tp', 'seq'), may hold values from 0.8192 to 16.384
- kernel_first: float32 [2, 3, 1024], P(None, None, 'tp'), may hold values from -27.1529 to 27.1529
- kernel_second: float32 [2, 3, 1024], P(None, None, 'tp'), may hold values from 0.8192 to 16.384
- gain_first: float32 [2, 2, 1024], P(None, None, 'tp'), may hold values from -27.1529 to 27.1529
- gain_second: float32 [2, 2, 1024], P(None, None, 'tp'), may hold values from 0.8192 to 16.384
Outputs:
- output: float32 [8192, 1024], P('seq', 'tp')
- input_grad: float32 [8192, 1024], P('seq', 'tp')
- entry_grad: float32 [2, 3, 1024, 1024], P(None, None, 'seq', 'tp')
- exit_grad: float32 [2, 1024, 1024], P(None, 'tp', 'seq')
- gate_grad: float32 [2, 2, 1024, 4608], P(None, None, 'seq', 'tp')
- down_grad: float32 [2, 4608, 1024], P(None, 'tp', 'seq')
- kernel_grad: float32 [2, 3, 1024], P(None, None, 'tp')
- gain_grad: float32 [2, 2, 1024], P(None, None, 'tp')
- entry_updated: float32 [2, 3, 1024, 1024], P(None, None, 'seq', 'tp')
- exit_updated: float32 [2, 1024, 1024], P(None, 'tp', 'seq')
- gate_updated: float32 [2, 2, 1024, 4608], P(None, None, 'seq', 'tp')
- down_updated: float32 [2, 4608, 1024], P(None, 'tp', 'seq')
- kernel_updated: float32 [2, 3, 1024], P(None, None, 'tp')
- gain_updated: float32 [2, 2, 1024], P(None, None, 'tp')
- entry_first_new: float32 [2, 3, 1024, 1024], P(None, None, 'seq', 'tp')
- entry_second_new: float32 [2, 3, 1024, 1024], P(None, None, 'seq', 'tp')
- exit_first_new: float32 [2, 1024, 1024], P(None, 'tp', 'seq')
- exit_second_new: float32 [2, 1024, 1024], P(None, 'tp', 'seq')
- gate_first_new: float32 [2, 2, 1024, 4608], P(None, None, 'seq', 'tp')
- gate_second_new: float32 [2, 2, 1024, 4608], P(None, None, 'seq', 'tp')
- down_first_new: float32 [2, 4608, 1024], P(None, 'tp', 'seq')
- down_second_new: float32 [2, 4608, 1024], P(None, 'tp', 'seq')
- kernel_first_new: float32 [2, 3, 1024], P(None, None, 'tp')
- kernel_second_new: float32 [2, 3, 1024], P(None, None, 'tp')
- gain_first_new: float32 [2, 2, 1024], P(None, None, 'tp')
- gain_second_new: float32 [2, 2, 1024], P(None, None, 'tp')
All inputs are finite; a program needn't handle non-finite values.
Results may differ from a plain program's by a relative error of at most 0.019.
The roundings to bfloat16 on the way count: a program that leaves them out, or rounds other values in their place, can miss the bound.
Values may be sent and summed in bfloat16 or wider, within the bound.
A program may use at most 192 MiB of HBM per device.

v0:
```python
import jax
import jax.numpy as jnp
from jax import lax
from jax.sharding import PartitionSpec as P

STEP = 4
EPS = 1e-06


def from_everyone(value, axis):
    copies = jnp.broadcast_to(value, (lax.axis_size(axis), *value.shape))
    return lax.all_to_all(copies, axis, split_axis=0, concat_axis=0, tiled=True)


def taken_together(value, axis):
    return from_everyone(value, axis).sum(axis=0)


def joined_along(blocks, dim):
    blocks = jnp.moveaxis(blocks, 0, dim)
    dims = blocks.shape
    return blocks.reshape(*dims[:dim], dims[dim] * dims[dim + 1], *dims[dim + 2 :])


def collect(value, axis, dim):
    return joined_along(from_everyone(value, axis), dim)


def cut_along(value, dim, peers):
    dims = value.shape
    blocks = value.reshape(*dims[:dim], peers, dims[dim] // peers, *dims[dim + 1 :])
    return jnp.moveaxis(blocks, dim, 0)


def sent_and_summed(value, axis, dim):
    peers = lax.axis_size(axis)
    blocks = lax.all_to_all(cut_along(value, dim, peers), axis, 0, 0, tiled=True)
    return jnp.sum(blocks, axis=0)


def from_behind(value, axis, by):
    peers = lax.axis_size(axis)
    pairs = [(i, i + by) for i in range(peers) if 0 <= i + by < peers]
    return lax.ppermute(value, axis, pairs)


def gather_turned(arrays, axis, dims):
    turned = [jnp.moveaxis(a, dim, 0) for a, dim in zip(arrays, dims)]
    widths = [t[0].size for t in turned]
    both = jnp.concatenate([t.reshape(-1, w) for t, w in zip(turned, widths)], axis=1)
    out = lax.all_gather(both, axis, axis=0, tiled=True)
    blocks = jnp.split(out, [sum(widths[:k]) for k in range(1, len(widths))], axis=1)
    return tuple(
        (
            jnp.moveaxis(b.reshape(-1, *t.shape[1:]), 0, dim)
            for b, t, dim in zip(blocks, turned, dims)
        )
    )


def packed_total(arrays, axis):
    ravelled, at, done = (jnp.concatenate([a.reshape(-1) for a in arrays]), 0, [])
    running = taken_together(ravelled, axis)
    for a in arrays:
        done.append(running[at : at + a.size].reshape(a.shape))
        at += a.size
    return tuple(done)


def bdot(left, right):
    return jnp.dot(left, right, preferred_element_type=jnp.float32)


def row_norm(value, width):
    sums = taken_together(jnp.sum(value * value, axis=1), "tp")
    scale = lax.rsqrt(sums / width + EPS)[:, None]
    return (value * scale, scale)


def norm_back(dnorm, normed, scale, gain, width):
    dnormed = dnorm * gain
    inner = taken_together(jnp.sum(dnormed * normed, axis=1), "tp")
    return (scale * (dnormed - normed * (inner / width)[:, None]), jnp.sum(dnorm * normed, axis=0))


def whole_rows(shard):
    return collect(shard, "tp", 1)


def whole_grads(shard):
    return collect(shard, "tp", 1)


def channel_sum(partial_value):
    return sent_and_summed(partial_value, "tp", 1)


def adamw(weight, grad, first, second, rate, decay):
    first_new = 0.9 * first + 0.1 * grad
    second_new = 0.999 * second + 0.001 * grad * grad
    update = first_new / (1.0 - 0.9**STEP) / (jnp.sqrt(second_new / (1.0 - 0.999**STEP)) + 1e-08)
    return (weight - rate * (update + decay * weight), first_new, second_new)


def layer_forward(hidden, entry, leave, gates, down, kern, gain, width):
    normed1, scale1 = row_norm(hidden, width)
    first_in = whole_rows((normed1 * gain[0]).astype(jnp.bfloat16))
    projected = jnp.einsum("td,cde->cte", first_in, entry, preferred_element_type=jnp.float32)
    b_part, c_part, x_part = (projected[0], projected[1], projected[2])
    product = b_part * x_part
    before = from_behind(product[-2:], "seq", 1)
    extended = jnp.concatenate([before, product], axis=0)
    conv_out = kern[0] * extended[:-2] + kern[1] * extended[1:-1] + kern[2] * extended[2:]
    gated = (c_part * conv_out).astype(jnp.bfloat16)
    mid = hidden + channel_sum(bdot(gated, leave))
    normed2, scale2 = row_norm(mid, width)
    second_in = whole_rows((normed2 * gain[1]).astype(jnp.bfloat16))
    gate_val = bdot(second_in, gates[0])
    up_val = bdot(second_in, gates[1])
    sig = jax.nn.sigmoid(gate_val)
    swish = gate_val * sig
    acted = (swish * up_val).astype(jnp.bfloat16)
    result = mid + channel_sum(bdot(acted, down))
    kept = (
        normed1,
        scale1,
        first_in,
        b_part,
        c_part,
        x_part,
        extended,
        conv_out,
        gated,
        normed2,
        scale2,
        second_in,
        gate_val,
        up_val,
        sig,
        swish,
        acted,
    )
    return (result, kept)


def layer_backward(grad, kept, entry, leave, gates, down, kern, gain, width):
    (
        normed1,
        scale1,
        first_in,
        b_part,
        c_part,
        x_part,
        extended,
        conv_out,
        gated,
        normed2,
        scale2,
        second_in,
        gate_val,
        up_val,
        sig,
        swish,
        acted,
    ) = kept
    grad_rows = whole_grads(grad.astype(jnp.bfloat16))
    dacted = bdot(grad_rows, down.T)
    down_g = bdot(acted.T, grad_rows)
    dgate = (dacted * up_val * sig * (1.0 + gate_val * (1.0 - sig))).astype(jnp.bfloat16)
    dup = (dacted * swish).astype(jnp.bfloat16)
    gate_g = jnp.stack([bdot(second_in.T, dgate), bdot(second_in.T, dup)])
    dnorm2 = channel_sum(bdot(dgate, gates[0].T) + bdot(dup, gates[1].T))
    back2, dgain2 = norm_back(dnorm2, normed2, scale2, gain[1], width)
    dmid = grad + back2
    mid_rows = whole_grads(dmid.astype(jnp.bfloat16))
    dgated = bdot(mid_rows, leave.T)
    exit_g = bdot(gated.T, mid_rows)
    dc_part = dgated * conv_out
    dconv = dgated * c_part
    kernel_g = jnp.stack(
        [
            jnp.sum(dconv * extended[:-2], axis=0),
            jnp.sum(dconv * extended[1:-1], axis=0),
            jnp.sum(dconv * extended[2:], axis=0),
        ]
    )
    channels = dconv.shape[1]
    zero_one = jnp.zeros((1, channels), jnp.float32)
    zero_two = jnp.zeros((2, channels), jnp.float32)
    dextended = (
        jnp.concatenate([kern[0] * dconv, zero_two], axis=0)
        + jnp.concatenate([zero_one, kern[1] * dconv, zero_one], axis=0)
        + jnp.concatenate([zero_two, kern[2] * dconv], axis=0)
    )
    returned = from_behind(dextended[:2], "seq", -1)
    tokens = dconv.shape[0]
    dproduct = dextended[2:] + jnp.concatenate(
        [jnp.zeros((tokens - 2, channels), jnp.float32), returned], axis=0
    )
    dproj = jnp.stack([dproduct * x_part, dc_part, dproduct * b_part]).astype(jnp.bfloat16)
    entry_g = jnp.einsum("td,cte->cde", first_in, dproj, preferred_element_type=jnp.float32)
    dnorm1 = channel_sum(
        jnp.einsum("cte,cde->td", dproj, entry, preferred_element_type=jnp.float32)
    )
    back1, dgain1 = norm_back(dnorm1, normed1, scale1, gain[0], width)
    return (dmid + back1, (entry_g, exit_g, gate_g, down_g), kernel_g, jnp.stack([dgain1, dgain2]))


def per_device(
    inputs,
    cotangent,
    entry_weight,
    exit_weight,
    gate_up,
    down_weight,
    conv_kernel,
    norm_gain,
    entry_first,
    entry_second,
    exit_first,
    exit_second,
    gate_first,
    gate_second,
    down_first,
    down_second,
    kernel_first,
    kernel_second,
    gain_first,
    gain_second,
):
    width = inputs.shape[1] * lax.axis_size("tp")
    layers = entry_weight.shape[0]
    rounded = (
        entry_weight.astype(jnp.bfloat16),
        exit_weight.astype(jnp.bfloat16),
        gate_up.astype(jnp.bfloat16),
        down_weight.astype(jnp.bfloat16),
    )
    gathered = gather_turned((rounded[0], rounded[1], rounded[2], rounded[3]), "seq", (2, 2, 2, 2))
    hidden = inputs
    kept_all = []
    for layer in range(layers):
        hidden, kept = layer_forward(
            hidden,
            gathered[0][layer],
            gathered[1][layer],
            gathered[2][layer],
            gathered[3][layer],
            conv_kernel[layer],
            norm_gain[layer],
            width,
        )
        kept_all.append(kept)
    grad = cotangent
    matrix_terms = [None] * layers
    kernel_terms = [None] * layers
    gain_terms = [None] * layers
    for layer in reversed(range(layers)):
        grad, terms, kernel_g, gain_g = layer_backward(
            grad,
            kept_all[layer],
            gathered[0][layer],
            gathered[1][layer],
            gathered[2][layer],
            gathered[3][layer],
            conv_kernel[layer],
            norm_gain[layer],
            width,
        )
        matrix_terms[layer] = terms
        kernel_terms[layer] = kernel_g
        gain_terms[layer] = gain_g
    stacked = tuple(
        (jnp.stack([matrix_terms[layer][index] for layer in range(layers)]) for index in range(4))
    )
    summed = lax.psum_scatter(stacked, "seq", scatter_dimension=2, tiled=True)
    kernel_grad, gain_grad = packed_total((jnp.stack(kernel_terms), jnp.stack(gain_terms)), "seq")
    entry_grad, exit_grad, gate_grad, down_grad = summed
    entry_u, entry_f, entry_s = adamw(
        entry_weight, entry_grad, entry_first, entry_second, 0.01, 0.1
    )
    exit_u, exit_f, exit_s = adamw(exit_weight, exit_grad, exit_first, exit_second, 0.01, 0.1)
    gate_u, gate_f, gate_s = adamw(gate_up, gate_grad, gate_first, gate_second, 0.01, 0.1)
    down_u, down_f, down_s = adamw(down_weight, down_grad, down_first, down_second, 0.01, 0.1)
    kernel_u, kernel_f, kernel_s = adamw(
        conv_kernel, kernel_grad, kernel_first, kernel_second, 0.2, 0.0
    )
    gain_u, gain_f, gain_s = adamw(norm_gain, gain_grad, gain_first, gain_second, 0.2, 0.0)
    return (
        hidden,
        grad,
        entry_grad,
        exit_grad,
        gate_grad,
        down_grad,
        kernel_grad,
        gain_grad,
        entry_u,
        exit_u,
        gate_u,
        down_u,
        kernel_u,
        gain_u,
        entry_f,
        entry_s,
        exit_f,
        exit_s,
        gate_f,
        gate_s,
        down_f,
        down_s,
        kernel_f,
        kernel_s,
        gain_f,
        gain_s,
    )


def solution(mesh):
    placed = (
        P("seq", "tp"),
        P("seq", "tp"),
        P(None, None, "seq", "tp"),
        P(None, "tp", "seq"),
        P(None, None, "seq", "tp"),
        P(None, "tp", "seq"),
        P(None, None, "tp"),
        P(None, None, "tp"),
        P(None, None, "seq", "tp"),
        P(None, None, "seq", "tp"),
        P(None, "tp", "seq"),
        P(None, "tp", "seq"),
        P(None, None, "seq", "tp"),
        P(None, None, "seq", "tp"),
        P(None, "tp", "seq"),
        P(None, "tp", "seq"),
        P(None, None, "tp"),
        P(None, None, "tp"),
        P(None, None, "tp"),
        P(None, None, "tp"),
    )
    return jax.shard_map(
        per_device,
        mesh=mesh,
        in_specs=placed,
        out_specs=(
            P("seq", "tp"),
            P("seq", "tp"),
            P(None, None, "seq", "tp"),
            P(None, "tp", "seq"),
            P(None, None, "seq", "tp"),
            P(None, "tp", "seq"),
            P(None, None, "tp"),
            P(None, None, "tp"),
            P(None, None, "seq", "tp"),
            P(None, "tp", "seq"),
            P(None, None, "seq", "tp"),
            P(None, "tp", "seq"),
            P(None, None, "tp"),
            P(None, None, "tp"),
            P(None, None, "seq", "tp"),
            P(None, None, "seq", "tp"),
            P(None, "tp", "seq"),
            P(None, "tp", "seq"),
            P(None, None, "seq", "tp"),
            P(None, None, "seq", "tp"),
            P(None, "tp", "seq"),
            P(None, "tp", "seq"),
            P(None, None, "tp"),
            P(None, None, "tp"),
            P(None, None, "tp"),
            P(None, None, "tp"),
        ),
        check_vma=False,
    )
```

profile of v0, /device:TPU:0, one launch (start us, length us, event | category | flops | bytes accessed | tf_op | source)
XLA Modules:
  0.0 816.9 jit_solution(14901821055226626452)
XLA Ops:
  11.7 5.4 all-to-all-start
  17.2 5.2 all-to-all-done
  26.9 8.2 %all-to-all-done.1 = bf16[4,256,256]{2,1,0:T(8,128)(2,1)S(1)} async-done(((bf16[4,256,256]{2,1,0:T(8,128)(2,1)}), bf16[4,256,256]{2,1,0:T(8,128)(2,1)S(1)}, u32[]{:S(2)}, u32[]{:S(2)}) %all-to-all-start.1) | async-done | bytes 524320 | tf_op jit(solution)/shard_map/all_to_all | solution.py:12
  36.8 52.9 %all-gather.2.cloned.1.call-done = bf16[1024,8960]{1,0:T(8,128)(2,1)} async-done(((bf16[32,8960]{1,0:T(8,128)(2,1)}), bf16[1024,8960]{1,0:T(8,128)(2,1)}) %all-gather.2.cloned.1.call-update) | async-done | bytes 18350096 | tf_op jit(solution)/shard_map/all_gather | solution.py:51
  107.0 20.4 %all_to_all.134 = f32[4,256,256]{2,1,0:T(8,128)S(1)} all-to-all(f32[4,256,256]{2,1,0:T(8,128)S(1)} %convolution_bitcast_fusion.16), channel_id=1, replica_groups=mesh['seq'=32,'tp'=4] {'tp'}, dimensions={0} | all-to-all | bytes 2097152 | tf_op jit(solution)/shard_map/all_to_all | solution.py:37
  131.5 7.9 split.18
  139.4 13.0 %reshape.240 = bf16[1024,2,2,1152]{3,2,1,0:T(2,128)(2,1)} reshape(bf16[1024,4608]{1,0:T(8,128)(2,1)} %split.18) | data formatting | bytes 18874368 | tf_op jit(solution)/shard_map/reshape | solution.py:55
  152.5 8.5 %copy.432 = bf16[1024,2,2,1152]{3,0,2,1:T(8,128)(2,1)} copy(bf16[1024,2,2,1152]{3,2,1,0:T(2,128)(2,1)} %reshape.240) | data formatting | bytes 18874368 | tf_op jit(solution)/shard_map/reshape | solution.py:55
  165.7 6.6 copy.342
  194.9 17.7 %all_to_all.135 = f32[4,256,256]{2,1,0:T(8,128)S(1)} all-to-all(f32[4,256,256]{2,1,0:T(8,128)S(1)} %convolution_bitcast_fusion.15), channel_id=1, replica_groups=mesh['seq'=32,'tp'=4] {'tp'}, dimensions={0} | all-to-all | bytes 2097152 | tf_op jit(solution)/shard_map/all_to_all | solution.py:37
  212.8 7.6 all_to_all.136
  220.6 10.9 %all_to_all.137 = bf16[4,256,256]{2,1,0:T(8,128)(2,1)S(1)} all-to-all(bf16[4,256,256]{2,1,0:T(8,128)(2,1)S(1)} %broadcast_in_dim.64), channel_id=1, replica_groups=mesh['seq'=32,'tp'=4] {'tp'}, dimensions={0} | all-to-all | bytes 1048576 | tf_op jit(solution)/shard_map/all_to_all | solution.py:12
  238.2 18.5 %all_to_all.138 = f32[4,256,256]{2,1,0:T(8,128)S(1)} all-to-all(f32[4,256,256]{2,1,0:T(8,128)S(1)} %convolution_bitcast_fusion.14), channel_id=1, replica_groups=mesh['seq'=32,'tp'=4] {'tp'}, dimensions={0} | all-to-all | bytes 2097152 | tf_op jit(solution)/shard_map/all_to_all | solution.py:37
  256.9 7.6 all_to_all.139
  269.2 8.9 %all-to-all-done.10 = bf16[4,256,256]{1,2,0:T(8,128)(2,1)S(1)} async-done(((bf16[4,256,256]{1,2,0:T(8,128)(2,1)}), bf16[4,256,256]{1,2,0:T(8,128)(2,1)S(1)}, u32[]{:S(2)}, u32[]{:S(2)}) %all-to-all-start.10) | async-done | bytes 524320 | tf_op jit(solution)/shard_map/all_to_all | solution.py:12
  311.6 6.4 all-to-all-done.13
  323.6 9.0 %all-to-all-done.11 = f32[4,256,256]{2,1,0:T(8,128)S(1)} async-done(((f32[4,256,256]{2,1,0:T(8,128)}), f32[4,256,256]{2,1,0:T(8,128)S(1)}, u32[]{:S(2)}, u32[]{:S(2)}) %all-to-all-start.11) | async-done | bytes 1048608 | tf_op jit(solution)/shard_map/all_to_all | solution.py:37
  343.9 10.5 %all_to_all.140 = bf16[4,256,256]{1,2,0:T(8,128)(2,1)S(1)} all-to-all(bf16[4,256,256]{1,2,0:T(8,128)(2,1)S(1)} %broadcast_in_dim.69), channel_id=1, replica_groups=mesh['seq'=32,'tp'=4] {'tp'}, dimensions={0} | all-to-all | bytes 1048576 | tf_op jit(solution)/shard_map/all_to_all | solution.py:12
  361.4 19.6 %all_to_all.141 = f32[4,256,256]{2,1,0:T(8,128)} all-to-all(f32[4,256,256]{2,1,0:T(8,128)S(1)} %convolution_bitcast_fusion.10), channel_id=1, replica_groups=mesh['seq'=32,'tp'=4] {'tp'}, dimensions={0} | all-to-all | bytes 2097152 | tf_op jit(solution)/shard_map/all_to_all | solution.py:37
  383.0 7.6 all_to_all.142
  392.4 11.2 %all_to_all.143 = bf16[4,256,256]{1,2,0:T(8,128)(2,1)S(1)} all-to-all(bf16[4,256,256]{1,2,0:T(8,128)(2,1)S(1)} %broadcast_in_dim.71), channel_id=1, replica_groups=mesh['seq'=32,'tp'=4] {'tp'}, dimensions={0} | all-to-all | bytes 1048576 | tf_op jit(solution)/shard_map/all_to_all | solution.py:12
  426.2 5.6 all-to-all-done.19
  448.3 9.4 %pad_maximum_fusion.1 = f32[2,1152,1024]{2,1,0:T(8,128)} fusion(f32[1,1152,1024]{2,1,0:T(8,128)} %convolution_bitcast_fusion, f32[1,1152,1024]{2,1,0:T(8,128)} %convolution_bitcast_fusion.1), kind=kLoop, calls=%fused_computation.3 | loop fusion | flops 2359296 | bytes 18874368 | tf_op jit(solution)/shard_map/stack | solution.py:274
  457.6 14.9 %copy.367 = f32[2,1152,1024]{1,0,2:T(2,128)} copy(f32[2,1152,1024]{2,1,0:T(8,128)} %pad_maximum_fusion.1) | data formatting | bytes 18874368 | tf_op jit(solution)/shard_map/stack | solution.py:274
  486.0 10.4 %copy.365 = f32[2,3,1024,256]{3,0,1,2:T(2,128)} copy(f32[2,3,1024,256]{2,3,1,0:T(8,128)} %pad_maximum_fusion.2) | data formatting | bytes 12582912 | tf_op jit(solution)/shard_map/stack | solution.py:274
  510.3 6.9 pad_maximum_fusion
  526.6 15.0 %all-to-all-done.22 = f32[4,256,256]{2,1,0:T(8,128)S(1)} async-done(((f32[4,256,256]{2,1,0:T(8,128)}), f32[4,256,256]{2,1,0:T(8,128)S(1)}, u32[]{:S(2)}, u32[]{:S(2)}) %all-to-all-start.22) | async-done | bytes 1048608 | tf_op jit(solution)/shard_map/all_to_all | solution.py:37
  545.9 5.2 all-to-all-done.23
  552.1 5.7 all-to-all-start.24
  558.7 9.7 %all-to-all-done.24 = f32[32,1,2560]{2,1,0:T(1,128)S(1)} async-done(((f32[32,1,2560]{2,1,0:T(1,128)}), f32[32,1,2560]{2,1,0:T(1,128)S(1)}, u32[]{:S(2)}, u32[]{:S(2)}) %all-to-all-start.24) | async-done | bytes 327712 | tf_op jit(solution)/shard_map/all_to_all | solution.py:12
  571.7 109.6 %all-reduce.12.cloned.1.call-done = (f32[2,3,1024,256]{3,0,1,2:T(2,128)}, f32[2,256,1024]{1,0,2:T(2,128)}, f32[2,1152,1024]{1,0,2:T(2,128)}) async-done(((f32[2,3,1024,256]{3,0,1,2:T(2,128)}, f32[2,256,1024]{1,0,2:T(2,128)}, f32[2,1152,1024]{1,0,2:T(2,128)}), (f32[2,3,1024,256]{3,0,1,2:T(2,128)}, f32[2,256,1024]{1,0,2:T(2,128)}, f32[2,1152,1024]{1,0,2:T(2,128)})) %all-reduce.12.cloned.1.call-update) | async-done | bytes 17825808
  686.9 120.7 %reduce-scatter.2.cloned.1.call-done = f32[2,2,32,1152]{3,2,1,0:T(8,128)} async-done(((f32[2,2,1024,1152]{3,2,1,0:T(8,128)}), f32[2,2,32,1152]{3,2,1,0:T(8,128)}) %reduce-scatter.2.cloned.1.call-update) | async-done | bytes 589840 | tf_op jit(solution)/shard_map/reduce_scatter | solution.py:276
  (418 shorter events, 223.6 us)
Async XLA Ops:
  7.2 82.4 %all-gather.2.cloned.1.call-start = ((), (), s32[]{:S(2)}) async-start(), calls=%async_computation.26 | async-start | bytes 18923520 | tf_op jit(solution)/shard_map/all_gather | solution.py:51
  11.7 10.7 %all-to-all-start = ((f32[4,1,256]{2,1,0:T(1,128)}), f32[4,1,256]{2,1,0:T(1,128)S(1)}, u32[]{:S(2)}, u32[]{:S(2)}) async-start(f32[4,1,256]{2,1,0:T(1,128)} %broadcast_in_dim.59), calls=%async_computation | async-start | bytes 8192 | tf_op jit(solution)/shard_map/all_to_all | solution.py:12
  17.1 155.3 %copy-start.78 = (f32[1,1,256]{2,1,0:T(1,128)}, f32[1,1,256]{2,1,0:T(1,128)S(1)}, u32[]{:S(2)}) copy-start(f32[1,1,256]{2,1,0:T(1,128)S(1)} %get-tuple-element.270) | copy-start | bytes 3076
  17.2 365.2 %copy-start.80 = (f32[1,1,256]{2,1,0:T(1,128)}, f32[1,1,256]{2,1,0:T(1,128)S(1)}, u32[]{:S(2)}) copy-start(f32[1,1,256]{2,1,0:T(1,128)S(1)} %get-tuple-element.269) | copy-start | bytes 3076
  23.4 11.8 %all-to-all-start.1 = ((bf16[4,256,256]{2,1,0:T(8,128)(2,1)}), bf16[4,256,256]{2,1,0:T(8,128)(2,1)S(1)}, u32[]{:S(2)}, u32[]{:S(2)}) async-start(bf16[4,256,256]{2,1,0:T(8,128)(2,1)} %broadcast_in_dim.60), calls=%async_computation.1 | async-start | bytes 1048576 | tf_op jit(solution)/shard_map/all_to_all | solution.py:12
  101.3 3.9 collective-permute-start
  128.3 44.1 %all-to-all-start.3 = ((f32[4,1,256]{2,1,0:T(1,128)}), f32[4,1,256]{2,1,0:T(1,128)S(1)}, u32[]{:S(2)}, u32[]{:S(2)}) async-start(f32[4,1,256]{2,1,0:T(1,128)} %broadcast_in_dim.61), calls=%async_computation.3 | async-start | bytes 8192 | tf_op jit(solution)/shard_map/all_to_all | solution.py:12
  173.5 14.0 %all-to-all-start.4 = ((bf16[4,256,256]{1,2,0:T(8,128)(2,1)}), bf16[4,256,256]{1,2,0:T(8,128)(2,1)S(1)}, u32[]{:S(2)}, u32[]{:S(2)}) async-start(bf16[4,256,256]{1,2,0:T(8,128)(2,1)} %broadcast_in_dim.62), calls=%async_computation.4 | async-start | bytes 1048576 | tf_op jit(solution)/shard_map/all_to_all | solution.py:12
  234.6 2.1 collective-permute-start.1
  265.6 12.5 %all-to-all-start.10 = ((bf16[4,256,256]{1,2,0:T(8,128)(2,1)}), bf16[4,256,256]{1,2,0:T(8,128)(2,1)S(1)}, u32[]{:S(2)}, u32[]{:S(2)}) async-start(bf16[4,256,256]{1,2,0:T(8,128)(2,1)} %broadcast_in_dim.66), calls=%async_computation.10 | async-start | bytes 1048576 | tf_op jit(solution)/shard_map/all_to_all | solution.py:12
  278.9 11.5 %all-to-all-start.12 = ((bf16[4,256,256]{1,2,0:T(8,128)(2,1)}), bf16[4,256,256]{1,2,0:T(8,128)(2,1)S(1)}, u32[]{:S(2)}, u32[]{:S(2)}) async-start(bf16[4,256,256]{1,2,0:T(8,128)(2,1)} %broadcast_in_dim.67), calls=%async_computation.12 | async-start | bytes 1048576 | tf_op jit(solution)/shard_map/all_to_all | solution.py:12
  301.4 16.6 %all-to-all-start.13 = ((f32[4,256,256]{2,1,0:T(8,128)}), f32[4,256,256]{2,1,0:T(8,128)}, u32[]{:S(2)}, u32[]{:S(2)}) async-start(f32[4,256,256]{2,1,0:T(8,128)} %bitcast.334), calls=%async_computation.13 | async-start | bytes 2097152 | tf_op jit(solution)/shard_map/all_to_all | solution.py:37
  318.0 14.6 %all-to-all-start.11 = ((f32[4,256,256]{2,1,0:T(8,128)}), f32[4,256,256]{2,1,0:T(8,128)S(1)}, u32[]{:S(2)}, u32[]{:S(2)}) async-start(f32[4,256,256]{2,1,0:T(8,128)} %convolution_bitcast_fusion.13), calls=%async_computation.11 | async-start | bytes 2097152 | tf_op jit(solution)/shard_map/all_to_all | solution.py:37
  333.2 8.5 %all-to-all-start.14 = ((f32[4,1,256]{2,1,0:T(1,128)}), f32[4,1,256]{2,1,0:T(1,128)S(1)}, u32[]{:S(2)}, u32[]{:S(2)}) async-start(f32[4,1,256]{2,1,0:T(1,128)} %broadcast_in_dim.68), calls=%async_computation.14 | async-start | bytes 8192 | tf_op jit(solution)/shard_map/all_to_all | solution.py:12
  356.8 3.2 collective-permute-start.2
  414.0 17.7 %all-to-all-start.19 = ((f32[4,256,256]{2,1,0:T(8,128)}), f32[4,256,256]{2,1,0:T(8,128)}, u32[]{:S(2)}, u32[]{:S(2)}) async-start(f32[4,256,256]{2,1,0:T(8,128)} %bitcast.369), calls=%async_computation.19 | async-start | bytes 2097152 | tf_op jit(solution)/shard_map/all_to_all | solution.py:37
  434.4 8.5 %all-to-all-start.20 = ((f32[4,1,256]{2,1,0:T(1,128)}), f32[4,1,256]{2,1,0:T(1,128)S(1)}, u32[]{:S(2)}, u32[]{:S(2)}) async-start(f32[4,1,256]{2,1,0:T(1,128)} %broadcast_in_dim.72), calls=%async_computation.20 | async-start | bytes 8192 | tf_op jit(solution)/shard_map/all_to_all | solution.py:12
  444.7 27.8 %all-to-all-start.21 = ((bf16[4,256,256]{1,2,0:T(8,128)(2,1)}), bf16[4,256,256]{1,2,0:T(8,128)(2,1)S(1)}, u32[]{:S(2)}, u32[]{:S(2)}) async-start(bf16[4,256,256]{1,2,0:T(8,128)(2,1)} %broadcast_in_dim.73), calls=%async_computation.21 | async-start | bytes 1048576 | tf_op jit(solution)/shard_map/all_to_all | solution.py:12
  448.3 233.0 %all-reduce.12.cloned.1.call-start = ((), (), s32[]{:S(2)}) async-start(), calls=%async_computation.28 | async-start | bytes 35651584
  475.9 3.9 collective-permute-start.3
  496.4 311.2 %reduce-scatter.2.cloned.1.call-start = ((), (), s32[]{:S(2)}) async-start(), calls=%async_computation.27 | async-start | bytes 19464192 | tf_op jit(solution)/shard_map/reduce_scatter | solution.py:276
  520.3 21.3 %all-to-all-start.22 = ((f32[4,256,256]{2,1,0:T(8,128)}), f32[4,256,256]{2,1,0:T(8,128)S(1)}, u32[]{:S(2)}, u32[]{:S(2)}) async-start(f32[4,256,256]{2,1,0:T(8,128)} %convolution_bitcast_fusion.9), calls=%async_computation.22 | async-start | bytes 2097152 | tf_op jit(solution)/shard_map/all_to_all | solution.py:37
  541.7 142.3 %copy-start.65 = (f32[2,256,32]{1,2,0:T(8,128)S(1)}, f32[2,256,32]{1,2,0:T(8,128)}, u32[]{:S(2)}) copy-start(f32[2,256,32]{1,2,0:T(8,128)} %param.23) | copy-start | bytes 196612
  541.7 142.3 %copy-start.68 = (f32[2,256,32]{1,2,0:T(8,128)S(1)}, f32[2,256,32]{1,2,0:T(8,128)}, u32[]{:S(2)}) copy-start(f32[2,256,32]{1,2,0:T(8,128)} %param.30) | copy-start | bytes 196612
  541.8 142.3 %copy-start.69 = (f32[2,256,32]{1,2,0:T(8,128)S(1)}, f32[2,256,32]{1,2,0:T(8,128)}, u32[]{:S(2)}) copy-start(f32[2,256,32]{1,2,0:T(8,128)} %param.31) | copy-start | bytes 196612
  541.8 143.1 %copy-start.49 = (f32[2,3,32,256]{3,2,1,0:T(8,128)S(1)}, f32[2,3,32,256]{3,2,1,0:T(8,128)}, u32[]{:S(2)}) copy-start(f32[2,3,32,256]{3,2,1,0:T(8,128)} %param.22) | copy-start | bytes 589828
  541.8 143.0 %copy-start.66 = (f32[2,3,32,256]{3,2,1,0:T(8,128)S(1)}, f32[2,3,32,256]{3,2,1,0:T(8,128)}, u32[]{:S(2)}) copy-start(f32[2,3,32,256]{3,2,1,0:T(8,128)} %param.28) | copy-start | bytes 589828
  541.8 143.0 %copy-start.67 = (f32[2,3,32,256]{3,2,1,0:T(8,128)S(1)}, f32[2,3,32,256]{3,2,1,0:T(8,128)}, u32[]{:S(2)}) copy-start(f32[2,3,32,256]{3,2,1,0:T(8,128)} %param.29) | copy-start | bytes 589828
  542.7 8.5 %all-to-all-start.23 = ((f32[4,1,256]{2,1,0:T(1,128)}), f32[4,1,256]{2,1,0:T(1,128)S(1)}, u32[]{:S(2)}, u32[]{:S(2)}) async-start(f32[4,1,256]{2,1,0:T(1,128)} %broadcast_in_dim.74), calls=%async_computation.23 | async-start | bytes 8192 | tf_op jit(solution)/shard_map/all_to_all | solution.py:12
  552.1 16.3 %all-to-all-start.24 = ((f32[32,1,2560]{2,1,0:T(1,128)}), f32[32,1,2560]{2,1,0:T(1,128)S(1)}, u32[]{:S(2)}, u32[]{:S(2)}) async-start(f32[32,1,2560]{2,1,0:T(1,128)} %broadcast_in_dim.75), calls=%async_computation.25 | async-start | bytes 655360 | tf_op jit(solution)/shard_map/all_to_all | solution.py:12
  557.8 128.0 %copy-start.37 = (f32[2,1152,32]{1,2,0:T(8,128)S(1)}, f32[2,1152,32]{1,2,0:T(8,128)}, u32[]{:S(2)}) copy-start(f32[2,1152,32]{1,2,0:T(8,128)} %param.25) | copy-start | bytes 884740
  557.8 128.0 %copy-start.62 = (f32[2,1152,32]{1,2,0:T(8,128)S(1)}, f32[2,1152,32]{1,2,0:T(8,128)}, u32[]{:S(2)}) copy-start(f32[2,1152,32]{1,2,0:T(8,128)} %param.34) | copy-start | bytes 884740
  (97 other events, 1976.2 us)
Sparse Core Ops, SparseCore 0:
  11.1 78.4 all-gather.1
  496.5 184.7 all-reduce.11
  685.8 121.7 reduce-scatter.1
where the time goes:
time: 829 us; the launch traced here: 817 us
  waiting for transfers between devices  366 us (44%)
  blocking collectives  132 us (16%)
  local copies, waits for them, and re-layouts  117 us (14%)
  starting transfers between devices  66.1 us (8%)
  matrix products  64.9 us (8%)
  other arithmetic  54.2 us (7%)
  between operations  16.5 us (2%)
    reduce_scatter x1, waiting for transfers between devices, per_device(): summed = lax.psum_scatter(stacked, 'seq', scatter_dimension=2, tiled=True)  121 us
    unnamed x4, waiting for transfers between devices  110 us
    all_to_all x4, blocking collectives, sent_and_summed(): lax.all_to_all(cut_along(value, dim, peers), axis, 0, 0, tiled=True)  76.1 us
    all_to_all x6, blocking collectives, from_everyone(): return lax.all_to_all(copies, axis, split_axis=0, concat_axis=0, tiled=True)  55.5 us
    dot_general x24, matrix products, bdot(): return jnp.dot(left, right, preferred_element_type=jnp.float32)  54.6 us
    all_gather x1, waiting for transfers between devices, gather_turned(): out = lax.all_gather(both, axis, axis=0, tiled=True)  52.9 us
    all_to_all x11, waiting for transfers between devices, from_everyone(): return lax.all_to_all(copies, axis, split_axis=0, concat_axis=0, tiled=True)  46.1 us
    all_to_all x11, starting transfers between devices, from_everyone(): return lax.all_to_all(copies, axis, split_axis=0, concat_axis=0, tiled=True)  42.7 us
  transfers between devices with their start and end apart: 22, of which 18 were waited for; matrix products, arithmetic and copies ran while one was open for 17% of the time, Pallas kernels for 0%

commit v1 on v0

--- a/solution.py
+++ b/solution.py
@@ -48,7 +48,9 @@
     turned = [jnp.moveaxis(a, dim, 0) for a, dim in zip(arrays, dims)]
     widths = [t[0].size for t in turned]
     both = jnp.concatenate([t.reshape(-1, w) for t, w in zip(turned, widths)], axis=1)
-    out = lax.all_gather(both, axis, axis=0, tiled=True)
+    out = jnp.concatenate(
+        lax.all_to_all(jnp.stack([both] * lax.axis_size(axis)), axis, 0, 0), axis=0
+    )
     blocks = jnp.split(out, [sum(widths[:k]) for k in range(1, len(widths))], axis=1)
     return tuple(
         (

time: 829 us -> 1080 us (1.30)
  waiting for transfers between devices: 366 us -> 570 us
  starting transfers between devices: 66.1 us -> 121 us
  blocking collectives: 132 us -> 111 us
  local copies, waits for them, and re-layouts: 117 us -> 130 us
    all_to_all x0 -> x1, waiting for transfers between devices: none -> 262 us  [gather_turned(): lax.all_to_all(jnp.stack([both] * lax.axis_size(axis)), axis, 0, 0)]
    all_gather x1 -> x0, waiting for transfers between devices: 52.9 us -> none  [gather_turned(): out = lax.all_gather(both, axis, axis=0, tiled=True)]
    ppermute x4, starting transfers between devices: 6.16 us -> 33.5 us  [from_behind(): return lax.ppermute(value, axis, pairs)]
    all_to_all x11, starting transfers between devices: 42.7 us -> 62.6 us  [from_everyone(): return lax.all_to_all(copies, axis, split_axis=0, concat_axis=0, tiled=True)]
    all_to_all x4, blocking collectives: 76.1 us -> 56.7 us  [sent_and_summed(): lax.all_to_all(cut_along(value, dim, peers), axis, 0, 0, tiled=True)]
    ppermute x4, waiting for transfers between devices: 0.94 us -> 12.2 us  [from_behind(): return lax.ppermute(value, axis, pairs)]
    split x9 -> x7, local copies, waits for them, and re-layouts: 24.6 us -> 28.9 us  [gather_turned(): jnp.split(out, [sum(widths[:k]) for k in range(1, len(widths))], axis=1)]
    unnamed x4 -> x3, waiting for transfers between devices: 110 us -> 110 us
  transfers between devices with their start and end apart: 22 -> 22, of which waited for: 18 -> 18; matrix products, arithmetic and copies ran while one was open for 17% -> 14% of each run, Pallas kernels for 0% -> 0%
where the time goes in v1:
time: 1080 us; the launch traced here: 1070 us
  waiting for transfers between devices  570 us (53%)
  local copies, waits for them, and re-layouts  130 us (12%)
  starting transfers between devices  121 us (11%)
  blocking collectives  111 us (10%)
  matrix products  64.8 us (6%)
  other arithmetic  56.5 us (5%)
  between operations  16.8 us (2%)
    all_to_all x1, waiting for transfers between devices, gather_turned(): lax.all_to_all(jnp.stack([both] * lax.axis_size(axis)), axis, 0, 0)  262 us
    reduce_scatter x1, waiting for transfers between devices, per_device(): summed = lax.psum_scatter(stacked, 'seq', scatter_dimension=2, tiled=True)  121 us
    unnamed x3, waiting for transfers between devices  110 us
    all_to_all x11, starting transfers between devices, from_everyone(): return lax.all_to_all(copies, axis, split_axis=0, concat_axis=0, tiled=True)  62.6 us
    all_to_all x4, blocking collectives, sent_and_summed(): lax.all_to_all(cut_along(value, dim, peers), axis, 0, 0, tiled=True)  56.7 us
    all_to_all x6, blocking collectives, from_everyone(): return lax.all_to_all(copies, axis, split_axis=0, concat_axis=0, tiled=True)  54.7 us
    dot_general x24, matrix products, bdot(): return jnp.dot(left, right, preferred_element_type=jnp.float32)  54.6 us
    all_to_all x11, waiting for transfers between devices, from_everyone(): return lax.all_to_all(copies, axis, split_axis=0, concat_axis=0, tiled=True)  39.4 us
  transfers between devices with their start and end apart: 22, of which 18 were waited for; matrix products, arithmetic and copies ran while one was open for 14% of the time, Pallas kernels for 0%

profile of v1, /device:TPU:0, one launch (start us, length us, event | category | flops | bytes accessed | tf_op | source)
XLA Modules:
  0.0 1070.7 jit_solution(4597683827903787434)
XLA Ops:
  8.9 5.4 all-to-all-start.1
  25.5 8.9 all-to-all-done.2
  34.4 6.7 stack.181
  41.1 7.6 all-to-all-start
  50.3 261.9 %all-to-all-done = bf16[32,32,8960]{2,1,0:T(8,128)(2,1)} async-done(((bf16[32,32,8960]{2,1,0:T(8,128)(2,1)}), bf16[32,32,8960]{2,1,0:T(8,128)(2,1)}, u32[]{:S(2)}, u32[]{:S(2)}) %all-to-all-start) | async-done | bytes 18350112 | tf_op jit(solution)/shard_map/all_to_all | solution.py:52
  335.0 13.3 %all_to_all.139 = f32[4,256,256]{2,1,0:T(8,128)S(1)} all-to-all(f32[4,256,256]{2,1,0:T(8,128)S(1)} %convolution_bitcast_fusion.16), channel_id=1, replica_groups=mesh['seq'=32,'tp'=4] {'tp'}, dimensions={0} | all-to-all | bytes 2097152 | tf_op jit(solution)/shard_map/all_to_all | solution.py:37
  352.4 7.9 split.18
  365.1 13.0 %reshape.246 = bf16[1024,2,2,1152]{3,2,1,0:T(2,128)(2,1)} reshape(bf16[1024,4608]{1,0:T(8,128)(2,1)} %split.18) | data formatting | bytes 18874368 | tf_op jit(solution)/shard_map/reshape | solution.py:57
  378.2 8.5 copy.486
  386.7 6.7 copy.396
  414.8 15.9 %all_to_all.140 = f32[4,256,256]{2,1,0:T(8,128)S(1)} all-to-all(f32[4,256,256]{2,1,0:T(8,128)S(1)} %convolution_bitcast_fusion.15), channel_id=1, replica_groups=mesh['seq'=32,'tp'=4] {'tp'}, dimensions={0} | all-to-all | bytes 2097152 | tf_op jit(solution)/shard_map/all_to_all | solution.py:37
  430.9 7.6 all_to_all.141
  438.7 10.5 all_to_all.142
  452.3 29.5 %collective-permute-start.1 = (f32[2,256]{1,0:T(2,128)S(1)}, f32[2,256]{1,0:T(2,128)S(1)}, u32[]{:S(2)}, u32[]{:S(2)}) collective-permute-start(f32[2,256]{1,0:T(2,128)S(1)} %slice.242), channel_id=1, source_target_pairs={{0,4},{4,8},{8,12},{12,16},{16,20},{20,24},{24,28},{28,32},{32,36}... | collective-permute-start | bytes 6152 | tf_op jit(solution)/shard_map/ppermute | solution.py:44
  484.0 13.3 %all_to_all.143 = f32[4,256,256]{2,1,0:T(8,128)S(1)} all-to-all(f32[4,256,256]{2,1,0:T(8,128)S(1)} %convolution_bitcast_fusion.14), channel_id=1, replica_groups=mesh['seq'=32,'tp'=4] {'tp'}, dimensions={0} | all-to-all | bytes 2097152 | tf_op jit(solution)/shard_map/all_to_all | solution.py:37
  497.5 7.7 all_to_all.144
  510.0 7.9 all-to-all-done.11
  562.0 9.0 all-to-all-done.12
  582.3 10.5 all_to_all.145
  602.2 14.2 %all_to_all.146 = f32[4,256,256]{2,1,0:T(8,128)} all-to-all(f32[4,256,256]{2,1,0:T(8,128)S(1)} %convolution_bitcast_fusion.10), channel_id=1, replica_groups=mesh['seq'=32,'tp'=4] {'tp'}, dimensions={0} | all-to-all | bytes 2097152 | tf_op jit(solution)/shard_map/all_to_all | solution.py:37
  618.4 7.7 all_to_all.147
  627.8 10.6 all_to_all.148
  680.6 9.4 pad_maximum_fusion.1
  690.0 14.9 %copy.421 = f32[2,1152,1024]{1,0,2:T(2,128)} copy(f32[2,1152,1024]{2,1,0:T(8,128)} %pad_maximum_fusion.1) | data formatting | bytes 18874368 | tf_op jit(solution)/shard_map/stack | solution.py:276
  712.2 8.8 collective-permute-done.3
  726.9 10.3 copy.419
  751.0 6.7 pad_maximum_fusion
  767.0 9.5 all-to-all-done.23
  787.0 24.2 %all-to-all-start.25 = ((f32[32,1,2560]{2,1,0:T(1,128)}), f32[32,1,2560]{2,1,0:T(1,128)S(1)}, u32[]{:S(2)}, u32[]{:S(2)}) async-start(f32[32,1,2560]{2,1,0:T(1,128)} %broadcast_in_dim.75), calls=%async_computation.26 | async-start | bytes 655360 | tf_op jit(solution)/shard_map/all_to_all | solution.py:12
  812.2 9.7 all-to-all-done.25
  825.2 109.6 %all-reduce.12.cloned.1.call-done = (f32[2,3,1024,256]{3,0,1,2:T(2,128)}, f32[2,256,1024]{1,0,2:T(2,128)}, f32[2,1152,1024]{1,0,2:T(2,128)}) async-done(((f32[2,3,1024,256]{3,0,1,2:T(2,128)}, f32[2,256,1024]{1,0,2:T(2,128)}, f32[2,1152,1024]{1,0,2:T(2,128)}), (f32[2,3,1024,256]{3,0,1,2:T(2,128)}, f32[2,256,1024]{1,0,2:T(2,128)}, f32[2,1152,1024]{1,0,2:T(2,128)})) %all-reduce.12.cloned.1.call-update) | async-done | bytes 17825808
  940.4 120.7 %reduce-scatter.2.cloned.1.call-done = f32[2,2,32,1152]{3,2,1,0:T(8,128)} async-done(((f32[2,2,1024,1152]{3,2,1,0:T(8,128)}), f32[2,2,32,1152]{3,2,1,0:T(8,128)}) %reduce-scatter.2.cloned.1.call-update) | async-done | bytes 589840 | tf_op jit(solution)/shard_map/reduce_scatter | solution.py:278
  (410 shorter events, 245.8 us)
Async XLA Ops:
  8.9 10.7 %all-to-all-start.1 = ((f32[4,1,256]{2,1,0:T(1,128)}), f32[4,1,256]{2,1,0:T(1,128)S(1)}, u32[]{:S(2)}, u32[]{:S(2)}) async-start(f32[4,1,256]{2,1,0:T(1,128)} %broadcast_in_dim.59), calls=%async_computation.1 | async-start | bytes 8192 | tf_op jit(solution)/shard_map/all_to_all | solution.py:12
  19.0 374.4 %copy-start.75 = (f32[1,1,256]{2,1,0:T(1,128)}, f32[1,1,256]{2,1,0:T(1,128)S(1)}, u32[]{:S(2)}) copy-start(f32[1,1,256]{2,1,0:T(1,128)S(1)} %get-tuple-element.296) | copy-start | bytes 3076
  19.0 598.7 %copy-start.77 = (f32[1,1,256]{2,1,0:T(1,128)}, f32[1,1,256]{2,1,0:T(1,128)S(1)}, u32[]{:S(2)}) copy-start(f32[1,1,256]{2,1,0:T(1,128)S(1)} %get-tuple-element.295) | copy-start | bytes 3076
  20.7 13.7 %all-to-all-start.2 = ((bf16[4,256,256]{2,1,0:T(8,128)(2,1)}), bf16[4,256,256]{2,1,0:T(8,128)(2,1)S(1)}, u32[]{:S(2)}, u32[]{:S(2)}) async-start(bf16[4,256,256]{2,1,0:T(8,128)(2,1)} %broadcast_in_dim.60), calls=%async_computation.2 | async-start | bytes 1048576 | tf_op jit(solution)/shard_map/all_to_all | solution.py:12
  41.1 271.1 %all-to-all-start = ((bf16[32,32,8960]{2,1,0:T(8,128)(2,1)}), bf16[32,32,8960]{2,1,0:T(8,128)(2,1)}, u32[]{:S(2)}, u32[]{:S(2)}) async-start(bf16[32,32,8960]{2,1,0:T(8,128)(2,1)} %stack.181), calls=%async_computation | async-start | bytes 36700160 | tf_op jit(solution)/shard_map/all_to_all | solution.py:52
  48.7 283.5 %copy-start.78 = (f32[1,1,256]{2,0,1:T(1,128)}, f32[1,1,256]{2,0,1:T(1,128)S(1)}, u32[]{:S(2)}) copy-start(f32[1,1,256]{2,0,1:T(1,128)S(1)} %get-tuple-element.290) | copy-start | bytes 3076
  48.7 283.5 %copy-start.80 = (f32[1,1,256]{2,0,1:T(1,128)}, f32[1,1,256]{2,0,1:T(1,128)S(1)}, u32[]{:S(2)}) copy-start(f32[1,1,256]{2,0,1:T(1,128)S(1)} %get-tuple-element.291) | copy-start | bytes 3076
  48.7 283.5 %copy-start.82 = (f32[1,1,256]{2,0,1:T(1,128)}, f32[1,1,256]{2,0,1:T(1,128)S(1)}, u32[]{:S(2)}) copy-start(f32[1,1,256]{2,0,1:T(1,128)S(1)} %get-tuple-element.292) | copy-start | bytes 3076
  326.3 5.9 collective-permute-start
  349.1 44.2 %all-to-all-start.4 = ((f32[4,1,256]{2,1,0:T(1,128)}), f32[4,1,256]{2,1,0:T(1,128)S(1)}, u32[]{:S(2)}, u32[]{:S(2)}) async-start(f32[4,1,256]{2,1,0:T(1,128)} %broadcast_in_dim.61), calls=%async_computation.4 | async-start | bytes 8192 | tf_op jit(solution)/shard_map/all_to_all | solution.py:12
  394.5 12.8 %all-to-all-start.5 = ((bf16[4,256,256]{1,2,0:T(8,128)(2,1)}), bf16[4,256,256]{1,2,0:T(8,128)(2,1)S(1)}, u32[]{:S(2)}, u32[]{:S(2)}) async-start(bf16[4,256,256]{1,2,0:T(8,128)(2,1)} %broadcast_in_dim.62), calls=%async_computation.5 | async-start | bytes 1048576 | tf_op jit(solution)/shard_map/all_to_all | solution.py:12
  452.3 30.3 %collective-permute-start.1 = (f32[2,256]{1,0:T(2,128)S(1)}, f32[2,256]{1,0:T(2,128)S(1)}, u32[]{:S(2)}, u32[]{:S(2)}) collective-permute-start(f32[2,256]{1,0:T(2,128)S(1)} %slice.242), channel_id=1, source_target_pairs={{0,4},{4,8},{8,12},{12,16},{16,20},{20,24},{24,28},{28,32},{32,36}... | collective-permute-start | bytes 6152 | tf_op jit(solution)/shard_map/ppermute | solution.py:44
  506.3 11.5 %all-to-all-start.11 = ((bf16[4,256,256]{1,2,0:T(8,128)(2,1)}), bf16[4,256,256]{1,2,0:T(8,128)(2,1)S(1)}, u32[]{:S(2)}, u32[]{:S(2)}) async-start(bf16[4,256,256]{1,2,0:T(8,128)(2,1)} %broadcast_in_dim.66), calls=%async_computation.11 | async-start | bytes 1048576 | tf_op jit(solution)/shard_map/all_to_all | solution.py:12
  518.7 11.5 %all-to-all-start.13 = ((bf16[4,256,256]{1,2,0:T(8,128)(2,1)}), bf16[4,256,256]{1,2,0:T(8,128)(2,1)S(1)}, u32[]{:S(2)}, u32[]{:S(2)}) async-start(bf16[4,256,256]{1,2,0:T(8,128)(2,1)} %broadcast_in_dim.67), calls=%async_computation.13 | async-start | bytes 1048576 | tf_op jit(solution)/shard_map/all_to_all | solution.py:12
  541.2 15.2 %all-to-all-start.14 = ((f32[4,256,256]{2,1,0:T(8,128)}), f32[4,256,256]{2,1,0:T(8,128)}, u32[]{:S(2)}, u32[]{:S(2)}) async-start(f32[4,256,256]{2,1,0:T(8,128)} %bitcast.335), calls=%async_computation.14 | async-start | bytes 2097152 | tf_op jit(solution)/shard_map/all_to_all | solution.py:37
  556.4 14.6 %all-to-all-start.12 = ((f32[4,256,256]{2,1,0:T(8,128)}), f32[4,256,256]{2,1,0:T(8,128)S(1)}, u32[]{:S(2)}, u32[]{:S(2)}) async-start(f32[4,256,256]{2,1,0:T(8,128)} %convolution_bitcast_fusion.13), calls=%async_computation.12 | async-start | bytes 2097152 | tf_op jit(solution)/shard_map/all_to_all | solution.py:37
  571.6 8.5 all-to-all-start.15
  595.2 5.6 collective-permute-start.2
  648.9 15.2 %all-to-all-start.20 = ((f32[4,256,256]{2,1,0:T(8,128)}), f32[4,256,256]{2,1,0:T(8,128)}, u32[]{:S(2)}, u32[]{:S(2)}) async-start(f32[4,256,256]{2,1,0:T(8,128)} %bitcast.370), calls=%async_computation.20 | async-start | bytes 2097152 | tf_op jit(solution)/shard_map/all_to_all | solution.py:37
  666.8 8.5 all-to-all-start.21
  677.1 27.8 %all-to-all-start.22 = ((bf16[4,256,256]{1,2,0:T(8,128)(2,1)}), bf16[4,256,256]{1,2,0:T(8,128)(2,1)S(1)}, u32[]{:S(2)}, u32[]{:S(2)}) async-start(bf16[4,256,256]{1,2,0:T(8,128)(2,1)} %broadcast_in_dim.73), calls=%async_computation.22 | async-start | bytes 1048576 | tf_op jit(solution)/shard_map/all_to_all | solution.py:12
  680.6 254.2 %all-reduce.12.cloned.1.call-start = ((), (), s32[]{:S(2)}) async-start(), calls=%async_computation.28 | async-start | bytes 35651584
  708.3 12.7 %collective-permute-start.3 = (f32[2,256]{1,0:T(2,128)}, f32[2,256]{1,0:T(2,128)}, u32[]{:S(2)}, u32[]{:S(2)}) collective-permute-start(f32[2,256]{1,0:T(2,128)} %slice.252), channel_id=1, source_target_pairs={{4,0},{8,4},{12,8},{16,12},{20,16},{24,20},{28,24},{32,28},{36,32}... | collective-permute-start | bytes 6152 | tf_op jit(solution)/shard_map/ppermute | solution.py:44
  737.3 323.8 %reduce-scatter.2.cloned.1.call-start = ((), (), s32[]{:S(2)}) async-start(), calls=%async_computation.27 | async-start | bytes 19464192 | tf_op jit(solution)/shard_map/reduce_scatter | solution.py:278
  760.9 15.6 %all-to-all-start.23 = ((f32[4,256,256]{2,1,0:T(8,128)}), f32[4,256,256]{2,1,0:T(8,128)S(1)}, u32[]{:S(2)}, u32[]{:S(2)}) async-start(f32[4,256,256]{2,1,0:T(8,128)} %convolution_bitcast_fusion.9), calls=%async_computation.23 | async-start | bytes 2097152 | tf_op jit(solution)/shard_map/all_to_all | solution.py:37
  776.6 161.0 %copy-start.63 = (f32[2,256,32]{1,2,0:T(8,128)S(1)}, f32[2,256,32]{1,2,0:T(8,128)}, u32[]{:S(2)}) copy-start(f32[2,256,32]{1,2,0:T(8,128)} %param.23) | copy-start | bytes 196612
  776.6 161.0 %copy-start.66 = (f32[2,256,32]{1,2,0:T(8,128)S(1)}, f32[2,256,32]{1,2,0:T(8,128)}, u32[]{:S(2)}) copy-start(f32[2,256,32]{1,2,0:T(8,128)} %param.30) | copy-start | bytes 196612
  776.6 161.7 %copy-start.48 = (f32[2,3,32,256]{3,2,1,0:T(8,128)S(1)}, f32[2,3,32,256]{3,2,1,0:T(8,128)}, u32[]{:S(2)}) copy-start(f32[2,3,32,256]{3,2,1,0:T(8,128)} %param.22) | copy-start | bytes 589828
  776.6 161.7 %copy-start.64 = (f32[2,3,32,256]{3,2,1,0:T(8,128)S(1)}, f32[2,3,32,256]{3,2,1,0:T(8,128)}, u32[]{:S(2)}) copy-start(f32[2,3,32,256]{3,2,1,0:T(8,128)} %param.28) | copy-start | bytes 589828
  776.7 161.7 %copy-start.65 = (f32[2,3,32,256]{3,2,1,0:T(8,128)S(1)}, f32[2,3,32,256]{3,2,1,0:T(8,128)}, u32[]{:S(2)}) copy-start(f32[2,3,32,256]{3,2,1,0:T(8,128)} %param.29) | copy-start | bytes 589828
  777.5 8.6 all-to-all-start.24
  787.0 34.8 %all-to-all-start.25 = ((f32[32,1,2560]{2,1,0:T(1,128)}), f32[32,1,2560]{2,1,0:T(1,128)S(1)}, u32[]{:S(2)}, u32[]{:S(2)}) async-start(f32[32,1,2560]{2,1,0:T(1,128)} %broadcast_in_dim.75), calls=%async_computation.26 | async-start | bytes 655360 | tf_op jit(solution)/shard_map/all_to_all | solution.py:12
  (92 other events, 2180.1 us)
Sparse Core Ops, SparseCore 0:
  737.4 197.3 all-reduce.11
  939.4 121.6 reduce-scatter.1
